TPU v7x, 32 devices: a whole 2x2x4 slice. The times are simulated.
32 devices in a mesh: ctx: 16 (over z, y, core), fsdp: 2 (over x).
Axes of the slice: x: 2, y: 2, z: 4, core: 2. Of those that a mesh axis runs over, the one named last changes fastest.
Arguments:
- tokens: bfloat16 [2, 2048, 1024], P('fsdp', 'ctx'), may hold values from -6 to 6
- w_qkv: bfloat16 [1024, 3072], P('fsdp'), may hold values from -0.1875 to 0.1875
- w_out: bfloat16 [1024, 1024], P('fsdp'), may hold values from -0.375 to 0.375
- w_up: bfloat16 [1024, 4096], P('fsdp'), may hold values from -0.1875 to 0.1875
- w_down: bfloat16 [4096, 1024], P('fsdp'), may hold values from -0.09375 to 0.09375
- w_time: bfloat16 [256, 2048], P('fsdp'), may hold values from -0.375 to 0.375
- gain_one: bfloat16 [1024], P('fsdp'), may hold values from 0.5 to 1.5
- bias_one: bfloat16 [1024], P('fsdp'), may hold values from -3 to 3
- gain_two: bfloat16 [1024], P('fsdp'), may hold values from 0.5 to 1.5
- bias_two: bfloat16 [1024], P('fsdp'), may hold values from -3 to 3
- bias_up: bfloat16 [4096], P('fsdp'), may hold values from -3 to 3
- bias_down: bfloat16 [1024], P('fsdp'), may hold values from -3 to 3
- lengths: int32 [2, 1], P('fsdp'), may hold values from 1024 to 2048, as said below
- time_steps: int32 [2, 1], P('fsdp'), may hold values from 0 to 999
- cotangent: bfloat16 [2, 2048, 1024], P('fsdp', 'ctx'), may hold values from -6 to 6
Outputs:
- output: bfloat16 [2, 2048, 1024], P('fsdp', 'ctx')
- grad_tokens: bfloat16 [2, 2048, 1024], P('fsdp', 'ctx')
- grad_qkv: float32 [1024, 3072], P('fsdp')
- grad_out: float32 [1024, 1024], P('fsdp')
- grad_up: float32 [1024, 4096], P('fsdp')
- grad_down: float32 [4096, 1024], P('fsdp')
- grad_time: float32 [256, 2048], P('fsdp')
- grad_gain_one: float32 [1024], P('fsdp')
- grad_bias_one: float32 [1024], P('fsdp')
- grad_gain_two: float32 [1024], P('fsdp')
- grad_bias_two: float32 [1024], P('fsdp')
- grad_bias_up: float32 [4096], P('fsdp')
- grad_bias_down: float32 [1024], P('fsdp')
Inputs may be any that keep to these rules, and one draw needn't show every extreme that they name: The 1 lengths of a group add up to at most 2048; the group's tokens after them are padding; in every group some sequence has the largest length.
All inputs are finite; a program needn't handle non-finite values.
Results may differ from a plain program's by a relative error of at most 0.025.
Values may be sent and summed in bfloat16 or wider, within the bound.
No kernel may reach another device: no remote copies, remote signals or barrier semaphores. Data moves between devices by JAX's collectives and lax.ppermute only.
A program may use at most 256 MiB of HBM per device.

v0:
```python
import math
import jax
import jax.numpy as jnp
from jax import lax
from jax.sharding import PartitionSpec as P

HEADS = 16
HIGH = lax.Precision.HIGHEST
EPSILON = 1e-05
NEGATIVE = -1e30


def layout(seq_lengths, offsets):
    ends = jnp.cumsum(seq_lengths)
    starts = jnp.concatenate([jnp.zeros((1,), jnp.int32), ends])
    segment = jnp.sum((offsets[:, None] >= ends[None, :]).astype(jnp.int32), axis=1)
    onehot = segment[:, None] == jnp.arange(seq_lengths.shape[0] + 1, dtype=jnp.int32)[None, :]
    begin = jnp.sum(jnp.where(onehot, starts[None, :], 0), axis=1)
    return (segment, onehot, offsets - begin)


def embed(steps_given, embed_width):
    half_width = embed_width // 2
    freq = jnp.exp(-math.log(10000.0) * jnp.arange(half_width, dtype=jnp.float32) / half_width)
    angle = steps_given.astype(jnp.float32)[..., None] * freq
    return jnp.concatenate([jnp.sin(angle), jnp.cos(angle)], axis=-1)


def rotary(values, position, heads):
    width = values.shape[-1]
    half_width = width // heads // 2
    inverse = jnp.exp(-math.log(10000.0) * jnp.arange(half_width, dtype=jnp.float32) / half_width)
    angle = position.astype(jnp.float32)[..., None] * inverse
    cosine = jnp.cos(angle)[..., None, :]
    sine = jnp.sin(angle)[..., None, :]
    split = values.reshape(values.shape[:-1] + (heads, 2, half_width))
    upper = split[..., 0, :]
    lower = split[..., 1, :]
    turned = jnp.stack([upper * cosine - lower * sine, lower * cosine + upper * sine], axis=-2)
    return turned.reshape(values.shape)


def normalize(values):
    centre = jnp.mean(values, axis=-1, keepdims=True)
    centered = values - centre
    spread = jnp.mean(centered * centered, axis=-1, keepdims=True)
    return centered * lax.rsqrt(spread + EPSILON)


def modulate(values, gain, bias, film_tok):
    width = values.shape[-1]
    return normalize(values) * (gain + film_tok[:, :width]) + (bias + film_tok[:, width:])


def affine(values, gain, bias):
    return normalize(values) * gain + bias


def gelu_exact(values):
    return jax.nn.gelu(values, approximate=False)


def split_heads(values, heads):
    return values.reshape(values.shape[0], heads, values.shape[1] // heads)


def contract_rows(left, right):
    return lax.dot_general(
        left, right, (((0,), (0,)), ((), ())), preferred_element_type=jnp.float32
    )


def contract_cols(left, right):
    return lax.dot_general(
        left, right, (((1,), (1,)), ((), ())), preferred_element_type=jnp.float32
    )


def body(
    tokens,
    w_qkv,
    w_out,
    w_up,
    w_down,
    w_time,
    gain_one,
    bias_one,
    gain_two,
    bias_two,
    bias_up,
    bias_down,
    lengths,
    time_steps,
    cotangent,
):
    gathered = (
        lax.all_gather(w_qkv, "fsdp", axis=0, tiled=True),
        lax.all_gather(w_out, "fsdp", axis=0, tiled=True),
        lax.all_gather(w_up, "fsdp", axis=0, tiled=True),
        lax.all_gather(w_down, "fsdp", axis=0, tiled=True),
        lax.all_gather(w_time, "fsdp", axis=0, tiled=True),
        lax.all_gather(gain_one, "fsdp", axis=0, tiled=True),
        lax.all_gather(bias_one, "fsdp", axis=0, tiled=True),
        lax.all_gather(gain_two, "fsdp", axis=0, tiled=True),
        lax.all_gather(bias_two, "fsdp", axis=0, tiled=True),
        lax.all_gather(bias_up, "fsdp", axis=0, tiled=True),
        lax.all_gather(bias_down, "fsdp", axis=0, tiled=True),
    )
    full_qkv, full_out, full_up, full_down, full_time = (
        gathered[0],
        gathered[1],
        gathered[2],
        gathered[3],
        gathered[4],
    )
    gain_first = gathered[5].astype(jnp.float32)
    bias_first = gathered[6].astype(jnp.float32)
    gain_second = gathered[7].astype(jnp.float32)
    bias_second = gathered[8].astype(jnp.float32)
    bias_hidden = gathered[9].astype(jnp.float32)
    bias_output = gathered[10].astype(jnp.float32)
    row_count = tokens.shape[1]
    width = tokens.shape[2]
    heads = HEADS
    head_size = width // heads
    scale = float(head_size) ** (-0.5)
    seq_lengths = lengths[0]
    seq_count = seq_lengths.shape[0]
    offsets = lax.axis_index("ctx") * row_count + jnp.arange(row_count, dtype=jnp.int32)
    segment, onehot, position = layout(seq_lengths, offsets)
    live = (segment < seq_count).astype(jnp.float32)
    onehot_float = onehot.astype(jnp.float32)
    inputs = tokens[0].astype(jnp.float32)
    temb = embed(time_steps[0], full_time.shape[0]).astype(jnp.bfloat16)
    film = jnp.dot(temb, full_time, preferred_element_type=jnp.float32)
    film_ext = jnp.concatenate([film, jnp.zeros((1, film.shape[1]), jnp.float32)], axis=0)
    film_tok = jnp.dot(onehot_float, film_ext, precision=HIGH)
    norm_one, pull_one = jax.vjp(modulate, inputs, gain_first, bias_first, film_tok)
    norm_one_b = norm_one.astype(jnp.bfloat16)
    mixed = jnp.dot(norm_one_b, full_qkv, preferred_element_type=jnp.float32)

    def turn_pair(query_raw, key_raw):
        return (rotary(query_raw, position, heads), rotary(key_raw, position, heads))

    turned, pull_turn = jax.vjp(turn_pair, mixed[:, :width], mixed[:, width : 2 * width])
    query = turned[0].astype(jnp.bfloat16)
    key = turned[1].astype(jnp.bfloat16)
    value = mixed[:, 2 * width :].astype(jnp.bfloat16)
    query_heads = split_heads(query, heads)
    key_heads = split_heads(key, heads)
    value_heads = split_heads(value, heads)
    row_max = jnp.full((heads, row_count), NEGATIVE, jnp.float32)
    weighted = jnp.zeros((row_count, heads, head_size), jnp.float32)
    piece_keys = lax.all_gather(key, "ctx", axis=0, tiled=True)
    piece_values = lax.all_gather(value, "ctx", axis=0, tiled=True)
    piece_rows = piece_keys.shape[0]
    piece_segment = layout(seq_lengths, jnp.arange(piece_rows, dtype=jnp.int32))[0]
    scaled = (
        jnp.einsum(
            "qhd,khd->hqk",
            query_heads,
            split_heads(piece_keys, heads),
            preferred_element_type=jnp.float32,
        )
        * scale
    )
    matches = (segment[:, None] == piece_segment[None, :])[None]
    masked = jnp.where(matches, scaled, NEGATIVE)
    new_max = jnp.maximum(row_max, jnp.max(masked, axis=2))
    weights_now = jnp.where(matches, jnp.exp(masked - new_max[:, :, None]), 0.0)
    decay = jnp.exp(row_max - new_max)
    row_sum = jnp.sum(weights_now, axis=2)
    partial_value = jnp.einsum(
        "hqk,khd->qhd",
        weights_now.astype(jnp.bfloat16),
        split_heads(piece_values, heads),
        preferred_element_type=jnp.float32,
    )
    weighted = weighted * decay.T[:, :, None] + partial_value
    row_max, row_sum, weighted = (new_max, row_sum, weighted)
    attended_heads = weighted / row_sum.T[:, :, None]
    log_total = row_max + jnp.log(row_sum)
    attended_b = attended_heads.reshape(row_count, width).astype(jnp.bfloat16)
    resid = inputs + jnp.dot(attended_b, full_out, preferred_element_type=jnp.float32)
    norm_two, pull_two = jax.vjp(affine, resid, gain_second, bias_second)
    norm_two_b = norm_two.astype(jnp.bfloat16)
    pre = jnp.dot(norm_two_b, full_up, preferred_element_type=jnp.float32) + bias_hidden
    act, pull_act = jax.vjp(gelu_exact, pre)
    act_b = act.astype(jnp.bfloat16)
    branch = jnp.dot(act_b, full_down, preferred_element_type=jnp.float32) + bias_output
    output = (live[:, None] * (resid + branch)).astype(jnp.bfloat16)
    again = (
        lax.all_gather(w_qkv, "fsdp", axis=0, tiled=True),
        lax.all_gather(w_out, "fsdp", axis=0, tiled=True),
        lax.all_gather(w_up, "fsdp", axis=0, tiled=True),
        lax.all_gather(w_down, "fsdp", axis=0, tiled=True),
        lax.all_gather(w_time, "fsdp", axis=0, tiled=True),
        lax.all_gather(gain_one, "fsdp", axis=0, tiled=True),
        lax.all_gather(bias_one, "fsdp", axis=0, tiled=True),
        lax.all_gather(gain_two, "fsdp", axis=0, tiled=True),
        lax.all_gather(bias_two, "fsdp", axis=0, tiled=True),
        lax.all_gather(bias_up, "fsdp", axis=0, tiled=True),
        lax.all_gather(bias_down, "fsdp", axis=0, tiled=True),
    )
    back_qkv, back_out, back_up, back_down = (again[0], again[1], again[2], again[3])
    grad_y = cotangent[0].astype(jnp.float32) * live[:, None]
    grad_bias_down = jnp.sum(grad_y, axis=0)
    grad_y_b = grad_y.astype(jnp.bfloat16)
    grad_down = contract_rows(act_b, grad_y_b)
    grad_act = contract_cols(grad_y_b, back_down)
    grad_pre = pull_act(grad_act)[0]
    grad_bias_up = jnp.sum(grad_pre, axis=0)
    grad_pre_b = grad_pre.astype(jnp.bfloat16)
    grad_up = contract_rows(norm_two_b, grad_pre_b)
    grad_norm_two = contract_cols(grad_pre_b, back_up)
    grad_resid_norm, grad_gain_two, grad_bias_two = pull_two(grad_norm_two)
    grad_resid = grad_y + grad_resid_norm
    grad_resid_b = grad_resid.astype(jnp.bfloat16)
    grad_out = contract_rows(attended_b, grad_resid_b)
    grad_att = contract_cols(grad_resid_b, back_out).astype(jnp.bfloat16)
    grad_att_heads = split_heads(grad_att, heads)
    delta = jnp.einsum(
        "qhd,qhd->hq", grad_att_heads.astype(jnp.float32), attended_heads, precision=HIGH
    )
    piece_keys = lax.all_gather(key, "ctx", axis=0, tiled=True)
    piece_values = lax.all_gather(value, "ctx", axis=0, tiled=True)
    piece_rows = piece_keys.shape[0]
    piece_segment = layout(seq_lengths, jnp.arange(piece_rows, dtype=jnp.int32))[0]
    keys_split = split_heads(piece_keys, heads)
    scaled = (
        jnp.einsum("qhd,khd->hqk", query_heads, keys_split, preferred_element_type=jnp.float32)
        * scale
    )
    matches = (segment[:, None] == piece_segment[None, :])[None]
    prob = jnp.where(matches, jnp.exp(scaled - log_total[:, :, None]), 0.0)
    grad_prob = jnp.einsum(
        "qhd,khd->hqk",
        grad_att_heads,
        split_heads(piece_values, heads),
        preferred_element_type=jnp.float32,
    )
    grad_score = (prob * (grad_prob - delta[:, :, None])).astype(jnp.bfloat16)
    grad_query = (
        jnp.einsum("hqk,khd->qhd", grad_score, keys_split, preferred_element_type=jnp.float32)
        * scale
    )
    stats_max, stats_delta = (
        lax.all_gather(log_total.T, "ctx", axis=0, tiled=True),
        lax.all_gather(delta.T, "ctx", axis=0, tiled=True),
    )
    piece_queries = lax.all_gather(query, "ctx", axis=0, tiled=True)
    piece_grads = lax.all_gather(grad_att, "ctx", axis=0, tiled=True)
    piece_rows = piece_queries.shape[0]
    piece_segment = layout(seq_lengths, jnp.arange(piece_rows, dtype=jnp.int32))[0]
    queries_split = split_heads(piece_queries, heads)
    grads_split = split_heads(piece_grads, heads)
    scaled = (
        jnp.einsum("qhd,khd->hqk", queries_split, key_heads, preferred_element_type=jnp.float32)
        * scale
    )
    matches = (piece_segment[:, None] == segment[None, :])[None]
    prob = jnp.where(matches, jnp.exp(scaled - stats_max.T[:, :, None]), 0.0)
    grad_value_now = jnp.einsum(
        "hqk,qhd->khd", prob.astype(jnp.bfloat16), grads_split, preferred_element_type=jnp.float32
    )
    grad_prob = jnp.einsum(
        "qhd,khd->hqk", grads_split, value_heads, preferred_element_type=jnp.float32
    )
    grad_score = (prob * (grad_prob - stats_delta.T[:, :, None])).astype(jnp.bfloat16)
    grad_key_now = (
        jnp.einsum("hqk,qhd->khd", grad_score, queries_split, preferred_element_type=jnp.float32)
        * scale
    )
    grad_turned = pull_turn(
        (grad_query.reshape(row_count, width), grad_key_now.reshape(row_count, width))
    )
    grad_mixed_b = jnp.concatenate(
        [grad_turned[0], grad_turned[1], grad_value_now.reshape(row_count, width)], axis=1
    ).astype(jnp.bfloat16)
    grad_qkv = contract_rows(norm_one_b, grad_mixed_b)
    grad_norm_one = contract_cols(grad_mixed_b, back_qkv)
    grad_inputs_norm, grad_gain_one, grad_bias_one, grad_film_tok = pull_one(grad_norm_one)
    grad_tokens = (grad_resid + grad_inputs_norm).astype(jnp.bfloat16)
    grad_film = lax.dot_general(
        onehot_float, grad_film_tok, (((0,), (0,)), ((), ())), precision=HIGH
    )[:seq_count]
    grad_time = lax.dot_general(
        temb.astype(jnp.float32), grad_film, (((0,), (0,)), ((), ())), precision=HIGH
    )
    shares = (
        lax.psum_scatter(
            grad_qkv.astype(jnp.bfloat16), "fsdp", scatter_dimension=0, tiled=True
        ).astype(jnp.float32),
        lax.psum_scatter(
            grad_out.astype(jnp.bfloat16), "fsdp", scatter_dimension=0, tiled=True
        ).astype(jnp.float32),
        lax.psum_scatter(
            grad_up.astype(jnp.bfloat16), "fsdp", scatter_dimension=0, tiled=True
        ).astype(jnp.float32),
        lax.psum_scatter(
            grad_down.astype(jnp.bfloat16), "fsdp", scatter_dimension=0, tiled=True
        ).astype(jnp.float32),
        lax.psum_scatter(
            grad_time.astype(jnp.bfloat16), "fsdp", scatter_dimension=0, tiled=True
        ).astype(jnp.float32),
        lax.psum_scatter(
            grad_gain_one.astype(jnp.bfloat16), "fsdp", scatter_dimension=0, tiled=True
        ).astype(jnp.float32),
        lax.psum_scatter(
            grad_bias_one.astype(jnp.bfloat16), "fsdp", scatter_dimension=0, tiled=True
        ).astype(jnp.float32),
        lax.psum_scatter(
            grad_gain_two.astype(jnp.bfloat16), "fsdp", scatter_dimension=0, tiled=True
        ).astype(jnp.float32),
        lax.psum_scatter(
            grad_bias_two.astype(jnp.bfloat16), "fsdp", scatter_dimension=0, tiled=True
        ).astype(jnp.float32),
        lax.psum_scatter(
            grad_bias_up.astype(jnp.bfloat16), "fsdp", scatter_dimension=0, tiled=True
        ).astype(jnp.float32),
        lax.psum_scatter(
            grad_bias_down.astype(jnp.bfloat16), "fsdp", scatter_dimension=0, tiled=True
        ).astype(jnp.float32),
    )
    (
        share_qkv,
        share_out,
        share_up,
        share_down,
        share_time,
        share_gone,
        share_bone,
        share_gtwo,
        share_btwo,
        share_bup,
        share_bdown,
    ) = shares
    totals = (
        lax.psum(share_qkv.astype(jnp.bfloat16), "ctx").astype(jnp.float32),
        lax.psum(share_out.astype(jnp.bfloat16), "ctx").astype(jnp.float32),
        lax.psum(share_up.astype(jnp.bfloat16), "ctx").astype(jnp.float32),
        lax.psum(share_down.astype(jnp.bfloat16), "ctx").astype(jnp.float32),
        lax.psum(share_time.astype(jnp.bfloat16), "ctx").astype(jnp.float32),
        lax.psum(share_gone.astype(jnp.bfloat16), "ctx").astype(jnp.float32),
        lax.psum(share_bone.astype(jnp.bfloat16), "ctx").astype(jnp.float32),
        lax.psum(share_gtwo.astype(jnp.bfloat16), "ctx").astype(jnp.float32),
        lax.psum(share_btwo.astype(jnp.bfloat16), "ctx").astype(jnp.float32),
        lax.psum(share_bup.astype(jnp.bfloat16), "ctx").astype(jnp.float32),
        lax.psum(share_bdown.astype(jnp.bfloat16), "ctx").astype(jnp.float32),
    )
    return (
        output[None],
        grad_tokens[None],
        totals[0],
        totals[1],
        totals[2],
        totals[3],
        totals[4],
        totals[5],
        totals[6],
        totals[7],
        totals[8],
        totals[9],
        totals[10],
    )


def solution(mesh):
    in_specs = (
        P("fsdp", "ctx", None),
        P("fsdp", None),
        P("fsdp", None),
        P("fsdp", None),
        P("fsdp", None),
        P("fsdp", None),
        P("fsdp"),
        P("fsdp"),
        P("fsdp"),
        P("fsdp"),
        P("fsdp"),
        P("fsdp"),
        P("fsdp", None),
        P("fsdp", None),
        P("fsdp", "ctx", None),
    )
    out_specs = (
        P("fsdp", "ctx", None),
        P("fsdp", "ctx", None),
        P("fsdp", None),
        P("fsdp", None),
        P("fsdp", None),
        P("fsdp", None),
        P("fsdp", None),
        P("fsdp"),
        P("fsdp"),
        P("fsdp"),
        P("fsdp"),
        P("fsdp"),
        P("fsdp"),
    )
    return jax.shard_map(body, mesh=mesh, in_specs=in_specs, out_specs=out_specs, check_vma=False)
```

profile of v0, /device:TPU:0, one launch (start us, length us, event | category | flops | bytes accessed | tf_op | source)
XLA Modules:
  0.0 1203.2 jit_solution(12869326752963828979)
XLA Ops:
  10.7 5.2 all-gather.1
  15.9 4.3 all-gather
  22.1 11.5 all-gather.15.cloned.1.call-done
  36.0 79.6 %all-gather.17.cloned.1.call-done = bf16[1024,3072]{1,0:T(8,128)(2,1)} async-done(((bf16[512,3072]{1,0:T(8,128)(2,1)}), bf16[1024,3072]{1,0:T(8,128)(2,1)}) %all-gather.17.cloned.1.call-update) | async-done | bytes 6291472 | tf_op jit(solution)/shard_map/all_gather | solution.py:97
  115.6 3.8 fusion.104
  120.5 2.0 copy.53
  122.5 2.0 copy.52
  124.5 2.0 multiply_subtract_fusion
  130.1 4.3 all_gather.67
  135.1 4.3 all-gather.3
  139.4 4.3 all-gather.2
  145.0 35.7 %all-gather.19.cloned.1.call-done = bf16[2048,1024]{0,1:T(8,128)(2,1)} async-done(((bf16[128,1024]{0,1:T(8,128)(2,1)}), bf16[2048,1024]{0,1:T(8,128)(2,1)}) %all-gather.19.cloned.1.call-update) | async-done | bytes 4194320 | tf_op jit(solution)/shard_map/all_gather | solution.py:154
  180.7 4.9 select_reduce_fusion
  185.6 5.0 fusion.1
  191.5 40.6 %all-gather.21.cloned.1.call-done = bf16[2048,1024]{1,0:T(8,128)(2,1)} async-done(((bf16[128,1024]{1,0:T(8,128)(2,1)}), bf16[2048,1024]{1,0:T(8,128)(2,1)}) %all-gather.21.cloned.1.call-update) | async-done | bytes 4194320 | tf_op jit(solution)/shard_map/all_gather | solution.py:155
  232.0 6.4 copy.54
  238.5 13.3 %fusion.100 = (bf16[128,16,64]{0,2,1:T(8,128)(2,1)S(1)}, f32[128,16,64]{0,2,1:T(8,128)}) fusion(f32[128,16]{0,1:T(8,128)S(1)} %bitcast.186, bf16[2048,16,64]{0,2,1:T(8,128)(2,1)} %bitcast.155, f32[16,128,2048]{2,1,0:T(8,128)} %copy-done, f32[16,128]{1,0:T(8,128)S(1)} %broadcast_maximum_fusion, pred[128,2048]{1,0:T(8,128)(4,1)S(1)} %broadcast_compare_fusion.1, ...), kind=kOutput, calls=%fused_computation.164 | convolution fusion | flops 558235648 | bytes 22044672 | tf_op jit(solution)/shard_map/hqk,khd->qhd/dot_general | solution.py:173
  251.8 13.3 %all-gather.23.cloned.1.call-done = bf16[1024,1024]{1,0:T(8,128)(2,1)} async-done(((bf16[512,1024]{1,0:T(8,128)(2,1)}), bf16[1024,1024]{1,0:T(8,128)(2,1)}) %all-gather.23.cloned.1.call-update) | async-done | bytes 2097168 | tf_op jit(solution)/shard_map/all_gather | solution.py:98
  265.1 2.1 fusion.101
  267.4 103.1 %all-gather.25.cloned.1.call-done = bf16[1024,4096]{1,0:T(8,128)(2,1)} async-done(((bf16[512,4096]{1,0:T(8,128)(2,1)}), bf16[1024,4096]{1,0:T(8,128)(2,1)}) %all-gather.25.cloned.1.call-update) | async-done | bytes 8388624 | tf_op jit(solution)/shard_map/all_gather | solution.py:99
  370.5 9.1 multiply_convert_fusion.5
  379.6 96.5 %all-gather.27.cloned.1.call-done = bf16[4096,1024]{1,0:T(8,128)(2,1)} async-done(((bf16[2048,1024]{1,0:T(8,128)(2,1)}), bf16[4096,1024]{1,0:T(8,128)(2,1)}) %all-gather.27.cloned.1.call-update) | async-done | bytes 8388624 | tf_op jit(solution)/shard_map/all_gather | solution.py:100
  476.1 10.8 fusion.102
  486.9 3.5 multiply_reduce_fusion
  499.8 23.5 %all_gather.71 = f32[2048,16]{0,1:T(8,128)} all-gather(f32[128,16]{0,1:T(8,128)S(1)} %get-tuple-element.63), channel_id=1, replica_groups=mesh['ctx'=16,'fsdp'=2] {'ctx'}, dimensions={0}, use_global_device_ids=true | all-gather | bytes 139264 | tf_op jit(solution)/shard_map/all_gather | solution.py:248
  524.5 19.3 %all_gather.73 = f32[2048,16]{0,1:T(8,128)} all-gather(f32[128,16]{0,1:T(8,128)S(1)} %bitcast.191), channel_id=1, replica_groups=mesh['ctx'=16,'fsdp'=2] {'ctx'}, dimensions={0}, use_global_device_ids=true | all-gather | bytes 139264 | tf_op jit(solution)/shard_map/all_gather | solution.py:249
  543.8 3.1 convolution_convert_fusion.3
  546.9 10.5 fusion.105
  557.4 14.4 %fusion.26 = f32[16,64,128]{2,1,0:T(8,128)} fusion(bf16[2048,16,64]{0,2,1:T(8,128)(2,1)} %bitcast.154, f32[16,128,2048]{2,1,0:T(8,128)} %copy-done, f32[16,128]{1,0:T(8,128)S(1)} %fusion.59, f32[16,128]{1,0:T(8,128)S(1)} %log_add_fusion, pred[128,2048]{1,0:T(8,128)(4,1)S(1)} %broadcast_compare_fusion.1, bf16[128,16,64]{0,2,1:T(8,128)(2,1)} %bitcast.166, ...), kind=kOutput, calls=%fused_computation.43 | convolution fusion | flops 1099038720 | bytes 26230784 | tf_op jit(solution)/shard_map/hqk,khd->qhd/dot_general | solution.py:244
  571.9 11.9 all-gather.31.cloned.1.call-done
  583.8 6.4 copy.56
  590.3 15.3 %multiply_convert_fusion.12 = bf16[16,2048,128]{2,1,0:T(8,128)(2,1)S(1)} fusion(f32[16,2048,128]{2,1,0:T(8,128)} %fusion.105, f32[16,2048]{1,0:T(8,128)} %bitcast.183, f32[16,2048]{1,0:T(8,128)S(1)} %bitcast.181, pred[2048,128]{1,0:T(8,128)(4,1)S(1)} %copy-done.23, bf16[2048,16,64]{0,2,1:T(8,128)(2,1)} %bitcast.157, ...), kind=kOutput, calls=%fused_computation.clone.clone.clone.clone.1 | convolution fusion | flops 562036736 | bytes 30146560 | tf_op jit(solution)/shard_map/qhd,khd->hqk/dot_general | solution.py:266
  608.6 11.1 fusion.34
  619.9 2.4 fusion.93
  625.3 5.9 convolution_convert_fusion.1
  632.1 5.8 convolution_convert_fusion
  638.9 4.5 convolution_convert_fusion.2
  644.2 102.0 %reduce-scatter.10.cloned.1.call-done = bf16[512,4096]{1,0:T(8,128)(2,1)} async-done(((bf16[1024,4096]{1,0:T(8,128)(2,1)}), bf16[512,4096]{1,0:T(8,128)(2,1)}) %reduce-scatter.10.cloned.1.call-update) | async-done | bytes 4194320 | tf_op jit(solution)/shard_map/reduce_scatter | solution.py:297
  746.2 102.2 %reduce-scatter.12.cloned.1.call-done = bf16[2048,1024]{1,0:T(8,128)(2,1)} async-done(((bf16[4096,1024]{1,0:T(8,128)(2,1)}), bf16[2048,1024]{1,0:T(8,128)(2,1)}) %reduce-scatter.12.cloned.1.call-update) | async-done | bytes 4194320 | tf_op jit(solution)/shard_map/reduce_scatter | solution.py:300
  848.4 79.8 %reduce-scatter.6.cloned.1.call-done = bf16[512,3072]{1,0:T(8,128)(2,1)} async-done(((bf16[1024,3072]{1,0:T(8,128)(2,1)}), bf16[512,3072]{1,0:T(8,128)(2,1)}) %reduce-scatter.6.cloned.1.call-update) | async-done | bytes 3145744 | tf_op jit(solution)/shard_map/reduce_scatter | solution.py:291
  928.9 4.3 all-gather.4
  935.2 5.5 fusion.37
  940.7 7.1 all-reduce.15
  948.2 35.4 %all-reduce.13 = (bf16[512]{0:T(512)(128)(2,1)S(1)}, bf16[512]{0:T(512)(128)(2,1)S(1)}, bf16[512]{0:T(512)(128)(2,1)S(1)}, bf16[512]{0:T(512)(128)(2,1)S(1)}, bf...) all-reduce(bf16[512]{0:T(512)(128)(2,1)S(1)} %dynamic-slice.1, ...), channel_id=1, replica_groups=mesh['ctx'=16,'fsdp'=2] {'ctx'}, use_global_device_ids=true, to_apply=%region_23.24 | all-reduce | flops 4608 | bytes 18432 | tf_op jit(solution)/shard_map/psum | solution.py:344
  988.0 191.4 %all-reduce.18.cloned.1.call-done = (bf16[512,3072]{1,0:T(8,128)(2,1)}, bf16[512,1024]{1,0:T(8,128)(2,1)}, bf16[512,4096]{1,0:T(8,128)(2,1)}, bf16[2048,1024]{1,0:T(8,128)(2,1)}, bf16[128,2048]{1,0:T(8,128)(2,1)}) async-done(((bf16[512,3072]{1,0:T(8,128)(2,1)}, bf16[512,1024]{1,0:T(8,128)(2,1)}, bf16[512,4096]{1,0:T(8,128)(2,1)}, bf16[2048,1024]{1,0:T(8,128)(2,1)}, bf16[128,2048]{1,0:T(8,128)(2,1)}), ...) | async-done | bytes 13107216 | tf_op jit(solution)/shard_map/psum | solution.py:339
  1179.4 5.5 convert_element_type.281
  1186.5 4.5 convert_element_type.285
  1191.0 4.4 convert_element_type.287
  (240 shorter events, 41.5 us)
Async XLA Ops:
  7.2 8.7 copy-start.56
  7.2 13.8 %copy-start.4 = (bf16[1,128,1024]{2,1,0:T(8,128)(2,1)S(1)}, bf16[1,128,1024]{2,1,0:T(8,128)(2,1)}, u32[]{:S(2)}) copy-start(bf16[1,128,1024]{2,1,0:T(8,128)(2,1)} %param.15) | copy-start | bytes 786436
  7.2 26.4 %all-gather.15.cloned.1.call-start = ((), (), s32[]{:S(2)}) async-start(), calls=%async_computation.5 | async-start | bytes 1572864 | tf_op jit(solution)/shard_map/all_gather | solution.py:101
  7.9 107.7 %all-gather.17.cloned.1.call-start = ((), (), s32[]{:S(2)}) async-start(), calls=%async_computation.6 | async-start | bytes 9437184 | tf_op jit(solution)/shard_map/all_gather | solution.py:97
  8.7 172.0 %all-gather.19.cloned.1.call-start = ((), (), s32[]{:S(2)}) async-start(), calls=%async_computation.7 | async-start | bytes 4456448 | tf_op jit(solution)/shard_map/all_gather | solution.py:154
  20.3 15.7 %copy-start.31 = (f32[2,1,512]{2,1,0:T(1,128)}, f32[2,1,512]{2,1,0:T(1,128)S(1)}, u32[]{:S(2)}) copy-start(f32[2,1,512]{2,1,0:T(1,128)S(1)} %convert_element_type.303) | copy-start | bytes 12292
  20.9 14.9 %copy-start.40 = (s32[128]{0:T(128)}, s32[128]{0:T(128)S(1)}, u32[]{:S(2)}) copy-start(s32[128]{0:T(128)S(1)} %get-tuple-element.44) | copy-start | bytes 1540
  21.1 98.3 %copy-start.47 = (f32[128]{0:T(128)}, f32[128]{0:T(128)S(1)}, u32[]{:S(2)}) copy-start(f32[128]{0:T(128)S(1)} %broadcast_multiply_fusion.1) | copy-start | bytes 1540
  21.3 98.1 %copy-start.53 = (f32[128]{0:T(128)}, f32[128]{0:T(128)S(1)}, u32[]{:S(2)}) copy-start(f32[128]{0:T(128)S(1)} %fusion.78) | copy-start | bytes 1540
  22.1 102.4 %copy-start.27 = (f32[128,32]{0,1:T(8,128)}, f32[128,32]{0,1:T(8,128)S(1)}, u32[]{:S(2)}) copy-start(f32[128,32]{0,1:T(8,128)S(1)} %get-tuple-element.65) | copy-start | bytes 49156
  127.3 104.7 %all-gather.21.cloned.1.call-start = ((), (), s32[]{:S(2)}) async-start(), calls=%async_computation.8 | async-start | bytes 4456448 | tf_op jit(solution)/shard_map/all_gather | solution.py:155
  128.1 137.0 %all-gather.23.cloned.1.call-start = ((), (), s32[]{:S(2)}) async-start(), calls=%async_computation.9 | async-start | bytes 3145728 | tf_op jit(solution)/shard_map/all_gather | solution.py:98
  128.7 241.8 %all-gather.25.cloned.1.call-start = ((), (), s32[]{:S(2)}) async-start(), calls=%async_computation.10 | async-start | bytes 12582912 | tf_op jit(solution)/shard_map/all_gather | solution.py:99
  129.3 5.8 copy-start.57
  129.3 10.1 copy-start.58
  129.3 14.5 %copy-start.41 = (s32[128]{0:T(128)S(1)}, s32[128]{0:T(128)}, u32[]{:S(2)}) copy-start(s32[128]{0:T(128)} %copy-done.40) | copy-start | bytes 1540
  129.3 14.7 %copy-start.21 = (bf16[128,16,1,32]{0,3,2,1:T(8,128)(2,1)S(1)}, bf16[128,16,1,32]{0,3,2,1:T(8,128)(2,1)}, u32[]{:S(2)}) copy-start(bf16[128,16,1,32]{0,3,2,1:T(8,128)(2,1)} %get-tuple-element.62) | copy-start | bytes 393220
  129.3 346.8 %all-gather.27.cloned.1.call-start = ((), (), s32[]{:S(2)}) async-start(), calls=%async_computation.11 | async-start | bytes 12582912 | tf_op jit(solution)/shard_map/all_gather | solution.py:100
  130.1 416.8 %all-gather.29.cloned.1.call-start = ((), (), s32[]{:S(2)}) async-start(), calls=%async_computation.12 | async-start | bytes 4456448 | tf_op jit(solution)/shard_map/all_gather | solution.py:251
  144.8 439.0 %all-gather.31.cloned.1.call-start = ((), (), s32[]{:S(2)}) async-start(), calls=%async_computation.13 | async-start | bytes 4456448 | tf_op jit(solution)/shard_map/all_gather | solution.py:252
  185.6 5.8 copy-start
  251.8 118.7 %copy-start.17 = (bf16[128,16,64]{0,2,1:T(8,128)(2,1)}, bf16[128,16,64]{0,2,1:T(8,128)(2,1)S(1)}, u32[]{:S(2)}) copy-start(bf16[128,16,64]{0,2,1:T(8,128)(2,1)S(1)} %get-tuple-element.69) | copy-start | bytes 786436
  251.8 118.7 %copy-start.33 = (f32[4096]{0:T(1024)S(1)}, f32[4096]{0:T(1024)}, u32[]{:S(2)}) copy-start(f32[4096]{0:T(1024)} %convert_element_type.264) | copy-start | bytes 49156
  267.2 223.2 %copy-start.36 = (f32[128]{0:T(128)}, f32[128]{0:T(128)S(1)}, u32[]{:S(2)}) copy-start(f32[128]{0:T(128)S(1)} %broadcast_multiply_fusion) | copy-start | bytes 1540
  267.4 223.0 %copy-start.38 = (f32[128]{0:T(128)}, f32[128]{0:T(128)S(1)}, u32[]{:S(2)}) copy-start(f32[128]{0:T(128)S(1)} %fusion.79) | copy-start | bytes 1540
  370.5 105.6 %copy-start.34 = (f32[128]{0:T(128)S(1)}, f32[128]{0:T(128)}, u32[]{:S(2)}) copy-start(f32[128]{0:T(128)} %get-tuple-element.43) | copy-start | bytes 1540
  476.1 10.8 copy-start.2
  494.5 149.0 %reduce-scatter.8.cloned.1.call-start = ((), (), s32[]{:S(2)}) async-start(), calls=%async_computation.15 | async-start | bytes 3145728 | tf_op jit(solution)/shard_map/reduce_scatter | solution.py:294
  571.8 18.4 %copy-start.23 = (pred[2048,128]{1,0:T(8,128)(4,1)S(1)}, pred[2048,128]{1,0:T(8,128)(4,1)}, u32[]{:S(2)}) copy-start(pred[2048,128]{1,0:T(8,128)(4,1)} %broadcast_compare_fusion) | copy-start | bytes 786436
  571.8 18.4 %copy-start.30 = (f32[2048,16]{0,1:T(8,128)S(1)}, f32[2048,16]{0,1:T(8,128)}, u32[]{:S(2)}) copy-start(f32[2048,16]{0,1:T(8,128)} %all_gather.71) | copy-start | bytes 393220
  571.9 72.3 %reduce-scatter.14.cloned.1.call-start = ((), (), s32[]{:S(2)}) async-start(), calls=%async_computation.18 | async-start | bytes 1572864 | tf_op jit(solution)/shard_map/reduce_scatter | solution.py:303
  590.3 15.3 %copy-start.1 = (bf16[2048,1024]{0,1:T(8,128)(2,1)S(1)}, bf16[2048,1024]{0,1:T(8,128)(2,1)}, u32[]{:S(2)}) copy-start(bf16[2048,1024]{0,1:T(8,128)(2,1)} %all-gather.29.cloned.1.call-done) | copy-start | bytes 12582916
  605.6 14.2 %slice-start = ((s8[6291456]{0:T(1024)(128)(4,1)}), s8[2097152]{0:T(1024)(128)(4,1)S(1)}, s32[]{:S(2)}) async-start(s8[6291456]{0:T(1024)(128)(4,1)} %bitcast.151), calls=%async_computation.20 | async-start | bytes 4194304
  608.6 11.2 copy-start.18
  608.6 11.2 slice-start.1
  608.6 11.2 copy-start.32
  608.6 11.2 copy-start.48
  625.0 121.2 %reduce-scatter.10.cloned.1.call-start = ((), (), s32[]{:S(2)}) async-start(), calls=%async_computation.16 | async-start | bytes 12582912 | tf_op jit(solution)/shard_map/reduce_scatter | solution.py:297
  631.2 217.2 %reduce-scatter.12.cloned.1.call-start = ((), (), s32[]{:S(2)}) async-start(), calls=%async_computation.17 | async-start | bytes 12582912 | tf_op jit(solution)/shard_map/reduce_scatter | solution.py:300
  637.9 290.3 %reduce-scatter.6.cloned.1.call-start = ((), (), s32[]{:S(2)}) async-start(), calls=%async_computation.14 | async-start | bytes 9437184 | tf_op jit(solution)/shard_map/reduce_scatter | solution.py:291
  643.5 535.9 %all-reduce.18.cloned.1.call-start = ((), (), s32[]{:S(2)}) async-start(), calls=%async_computation.19 | async-start | bytes 26214400 | tf_op jit(solution)/shard_map/psum | solution.py:339
  935.2 5.5 copy-start.43
  935.2 5.5 copy-start.44
  935.2 51.9 %copy-start.6 = (f32[128,1024]{1,0:T(8,128)S(1)}, f32[128,1024]{1,0:T(8,128)}, u32[]{:S(2)}) copy-start(f32[128,1024]{1,0:T(8,128)} %copy-done.5) | copy-start | bytes 1572868
  935.2 51.9 %copy-start.15 = (f32[128,1024]{1,0:T(8,128)S(1)}, f32[128,1024]{1,0:T(8,128)}, u32[]{:S(2)}) copy-start(f32[128,1024]{1,0:T(8,128)} %get-tuple-element.48) | copy-start | bytes 1572868
  935.2 51.9 %copy-start.52 = (f32[128]{0:T(128)S(1)}, f32[128]{0:T(128)}, u32[]{:S(2)}) copy-start(f32[128]{0:T(128)} %copy-done.51) | copy-start | bytes 1540
  1179.4 5.5 copy-start.16
  1179.4 7.1 copy-start.8
  (33 other events, 81.0 us)
Sparse Core Ops, SparseCore 0:
  9.6 23.9 all-gather.14
  35.2 80.4 all-gather.16
  127.4 53.2 all-gather.18
  183.3 48.7 all-gather.20
  233.4 31.5 all-gather.22
  266.5 103.9 all-gather.24
  372.0 103.9 all-gather.26
  478.8 54.0 all-gather.28
  535.0 48.7 all-gather.30
  586.5 30.2 reduce-scatter.7
  625.1 18.9 reduce-scatter.13
  646.9 99.2 reduce-scatter.9
  749.1 99.2 reduce-scatter.11
  851.1 77.0 reduce-scatter.5
  933.9 245.5 all-reduce.17
where the time goes:
time: 1210 us; the launch traced here: 1200 us
  waiting for transfers between devices  872 us (72%)
  matrix products  132 us (11%)
  blocking collectives  112 us (9%)
  other arithmetic  40 us (3%)
  local copies, waits for them, and re-layouts  29.2 us (2%)
  between operations  17.5 us (1%)
    psum x1, waiting for transfers between devices, body(): lax.psum(share_qkv.astype(jnp.bfloat16), 'ctx').astype(jnp.float32)  191 us
    all_gather x1, waiting for transfers between devices, body(): lax.all_gather(w_up, 'fsdp', axis=0, tiled=True)  103 us
    reduce_scatter x1, waiting for transfers between devices, body(): lax.psum_scatter(grad_down.astype(jnp.bfloat16), 'fsdp', scatter_dimensio...  102 us
    reduce_scatter x1, waiting for transfers between devices, body(): lax.psum_scatter(grad_up.astype(jnp.bfloat16), 'fsdp', scatter_dimension=...  102 us
    all_gather x1, waiting for transfers between devices, body(): lax.all_gather(w_down, 'fsdp', axis=0, tiled=True)  96.5 us
    reduce_scatter x1, waiting for transfers between devices, body(): lax.psum_scatter(grad_qkv.astype(jnp.bfloat16), 'fsdp', scatter_dimension...  79.8 us
    all_gather x1, waiting for transfers between devices, body(): lax.all_gather(w_qkv, 'fsdp', axis=0, tiled=True)  79.6 us
    all_gather x1, waiting for transfers between devices, body(): piece_values = lax.all_gather(value, 'ctx', axis=0, tiled=True)  40.6 us
  transfers between devices with their start and end apart: 15, of which 13 were waited for; matrix products, arithmetic and copies ran while one was open for 14% of the time, Pallas kernels for 0%

commit v1 on v0

--- a/solution.py
+++ b/solution.py
@@ -336,7 +336,7 @@
         share_bdown,
     ) = shares
     totals = (
-        lax.psum(share_qkv.astype(jnp.bfloat16), "ctx").astype(jnp.float32),
+        jnp.sum(lax.all_gather(share_qkv.astype(jnp.bfloat16), "ctx"), axis=0).astype(jnp.float32),
         lax.psum(share_out.astype(jnp.bfloat16), "ctx").astype(jnp.float32),
         lax.psum(share_up.astype(jnp.bfloat16), "ctx").astype(jnp.float32),
         lax.psum(share_down.astype(jnp.bfloat16), "ctx").astype(jnp.float32),

time: 1210 us -> 1410 us (1.17)
  waiting for transfers between devices: 872 us -> 1050 us
  other arithmetic: 40 us -> 61.2 us
    all_gather x0 -> x1, waiting for transfers between devices: none -> 232 us  [body(): lax.all_gather(share_qkv.astype(jnp.bfloat16), 'ctx')]
    psum x1, waiting for transfers between devices: 191 us -> 141 us  [body(): lax.psum(share_out.astype(jnp.bfloat16), 'ctx').astype(jnp.float32)]
    reduce_sum x0 -> x1, other arithmetic: none -> 17 us  [body(): jnp.sum(lax.all_gather(share_qkv.astype(jnp.bfloat16), 'ctx'), axis=0)]
  transfers between devices with their start and end apart: 15 -> 16, of which waited for: 13 -> 14; matrix products, arithmetic and copies ran while one was open for 14% -> 13% of each run, Pallas kernels for 0% -> 0%
where the time goes in v1:
time: 1410 us; the launch traced here: 1400 us
  waiting for transfers between devices  1050 us (74%)
  matrix products  129 us (9%)
  blocking collectives  113 us (8%)
  other arithmetic  61.2 us (4%)
  local copies, waits for them, and re-layouts  27.7 us (2%)
  between operations  17.7 us (1%)
    all_gather x1, waiting for transfers between devices, body(): lax.all_gather(share_qkv.astype(jnp.bfloat16), 'ctx')  232 us
    psum x1, waiting for transfers between devices, body(): lax.psum(share_out.astype(jnp.bfloat16), 'ctx').astype(jnp.float32)  141 us
    all_gather x1, waiting for transfers between devices, body(): lax.all_gather(w_up, 'fsdp', axis=0, tiled=True)  103 us
    reduce_scatter x1, waiting for transfers between devices, body(): lax.psum_scatter(grad_down.astype(jnp.bfloat16), 'fsdp', scatter_dimensio...  102 us
    reduce_scatter x1, waiting for transfers between devices, body(): lax.psum_scatter(grad_up.astype(jnp.bfloat16), 'fsdp', scatter_dimension=...  102 us
    all_gather x1, waiting for transfers between devices, body(): lax.all_gather(w_down, 'fsdp', axis=0, tiled=True)  96.5 us
    reduce_scatter x1, waiting for transfers between devices, body(): lax.psum_scatter(grad_qkv.astype(jnp.bfloat16), 'fsdp', scatter_dimension...  79.7 us
    all_gather x1, waiting for transfers between devices, body(): lax.all_gather(w_qkv, 'fsdp', axis=0, tiled=True)  79.6 us
  transfers between devices with their start and end apart: 16, of which 14 were waited for; matrix products, arithmetic and copies ran while one was open for 13% of the time, Pallas kernels for 0%

profile of v1, /device:TPU:0, one launch (start us, length us, event | category | flops | bytes accessed | tf_op | source)
XLA Modules:
  0.0 1401.5 jit_solution(8347317866701322425)
XLA Ops:
  10.7 5.2 all-gather.2
  15.9 4.3 all-gather.1
  22.1 11.5 all-gather.17.cloned.1.call-done
  36.0 79.6 %all-gather.19.cloned.1.call-done = bf16[1024,3072]{1,0:T(8,128)(2,1)} async-done(((bf16[512,3072]{1,0:T(8,128)(2,1)}), bf16[1024,3072]{1,0:T(8,128)(2,1)}) %all-gather.19.cloned.1.call-update) | async-done | bytes 6291472 | tf_op jit(solution)/shard_map/all_gather | solution.py:97
  115.6 3.8 fusion.104
  130.1 4.3 all_gather.73
  135.1 4.3 all-gather.4
  139.4 4.3 all-gather.3
  145.0 35.7 %all-gather.21.cloned.1.call-done = bf16[2048,1024]{0,1:T(8,128)(2,1)} async-done(((bf16[128,1024]{0,1:T(8,128)(2,1)}), bf16[2048,1024]{0,1:T(8,128)(2,1)}) %all-gather.21.cloned.1.call-update) | async-done | bytes 4194320 | tf_op jit(solution)/shard_map/all_gather | solution.py:154
  180.7 4.9 select_reduce_fusion
  185.6 5.0 fusion.1
  191.5 40.6 %all-gather.23.cloned.1.call-done = bf16[2048,1024]{1,0:T(8,128)(2,1)} async-done(((bf16[128,1024]{1,0:T(8,128)(2,1)}), bf16[2048,1024]{1,0:T(8,128)(2,1)}) %all-gather.23.cloned.1.call-update) | async-done | bytes 4194320 | tf_op jit(solution)/shard_map/all_gather | solution.py:155
  232.0 6.4 copy.54
  238.5 13.3 fusion.100
  251.8 13.3 all-gather.25.cloned.1.call-done
  265.1 2.1 fusion.101
  267.4 103.1 %all-gather.27.cloned.1.call-done = bf16[1024,4096]{1,0:T(8,128)(2,1)} async-done(((bf16[512,4096]{1,0:T(8,128)(2,1)}), bf16[1024,4096]{1,0:T(8,128)(2,1)}) %all-gather.27.cloned.1.call-update) | async-done | bytes 8388624 | tf_op jit(solution)/shard_map/all_gather | solution.py:99
  370.5 9.1 multiply_convert_fusion.5
  379.6 96.5 %all-gather.29.cloned.1.call-done = bf16[4096,1024]{1,0:T(8,128)(2,1)} async-done(((bf16[2048,1024]{1,0:T(8,128)(2,1)}), bf16[4096,1024]{1,0:T(8,128)(2,1)}) %all-gather.29.cloned.1.call-update) | async-done | bytes 8388624 | tf_op jit(solution)/shard_map/all_gather | solution.py:100
  476.1 10.8 fusion.102
  486.9 3.5 multiply_reduce_fusion
  499.8 23.5 %all_gather.77 = f32[2048,16]{0,1:T(8,128)} all-gather(f32[128,16]{0,1:T(8,128)S(1)} %get-tuple-element.62), channel_id=1, replica_groups=mesh['ctx'=16,'fsdp'=2] {'ctx'}, dimensions={0}, use_global_device_ids=true | all-gather | bytes 139264 | tf_op jit(solution)/shard_map/all_gather | solution.py:248
  524.6 19.3 %all_gather.79 = f32[2048,16]{0,1:T(8,128)} all-gather(f32[128,16]{0,1:T(8,128)S(1)} %bitcast.195), channel_id=1, replica_groups=mesh['ctx'=16,'fsdp'=2] {'ctx'}, dimensions={0}, use_global_device_ids=true | all-gather | bytes 139264 | tf_op jit(solution)/shard_map/all_gather | solution.py:249
  543.9 3.0 convolution_convert_fusion.3
  546.9 10.5 fusion.105
  557.4 14.4 %fusion.26 = f32[16,64,128]{2,1,0:T(8,128)} fusion(bf16[2048,16,64]{0,2,1:T(8,128)(2,1)} %bitcast.158, f32[16,128,2048]{2,1,0:T(8,128)} %copy-done, f32[16,128]{1,0:T(8,128)S(1)} %fusion.59, f32[16,128]{1,0:T(8,128)S(1)} %log_add_fusion, pred[128,2048]{1,0:T(8,128)(4,1)S(1)} %broadcast_compare_fusion.1, bf16[128,16,64]{0,2,1:T(8,128)(2,1)} %bitcast.170, ...), kind=kOutput, calls=%fused_computation.43 | convolution fusion | flops 1099038720 | bytes 26230784 | tf_op jit(solution)/shard_map/hqk,khd->qhd/dot_general | solution.py:244
  572.0 12.0 all-gather.33.cloned.1.call-done
  583.9 6.4 copy.56
  590.4 15.8 %multiply_convert_fusion.12 = bf16[16,2048,128]{2,1,0:T(8,128)(2,1)S(1)} fusion(f32[16,2048,128]{2,1,0:T(8,128)} %fusion.105, f32[16,2048]{1,0:T(8,128)} %bitcast.187, f32[16,2048]{1,0:T(8,128)S(1)} %bitcast.185, pred[2048,128]{1,0:T(8,128)(4,1)S(1)} %copy-done.19, bf16[2048,16,64]{0,2,1:T(8,128)(2,1)} %bitcast.161, ...), kind=kOutput, calls=%fused_computation.clone.clone.clone.clone.1 | convolution fusion | flops 562036736 | bytes 30146560 | tf_op jit(solution)/shard_map/qhd,khd->hqk/dot_general | solution.py:266
  609.6 7.4 fusion.34
  617.1 2.4 fusion.93
  622.5 5.9 convolution_convert_fusion.1
  629.4 5.8 convolution_convert_fusion
  636.2 4.5 convolution_convert_fusion.2
  641.5 102.0 %reduce-scatter.10.cloned.1.call-done = bf16[512,4096]{1,0:T(8,128)(2,1)} async-done(((bf16[1024,4096]{1,0:T(8,128)(2,1)}), bf16[512,4096]{1,0:T(8,128)(2,1)}) %reduce-scatter.10.cloned.1.call-update) | async-done | bytes 4194320 | tf_op jit(solution)/shard_map/reduce_scatter | solution.py:297
  743.5 102.3 %reduce-scatter.12.cloned.1.call-done = bf16[2048,1024]{1,0:T(8,128)(2,1)} async-done(((bf16[4096,1024]{1,0:T(8,128)(2,1)}), bf16[2048,1024]{1,0:T(8,128)(2,1)}) %reduce-scatter.12.cloned.1.call-update) | async-done | bytes 4194320 | tf_op jit(solution)/shard_map/reduce_scatter | solution.py:300
  845.8 79.7 %reduce-scatter.6.cloned.1.call-done = bf16[512,3072]{1,0:T(8,128)(2,1)} async-done(((bf16[1024,3072]{1,0:T(8,128)(2,1)}), bf16[512,3072]{1,0:T(8,128)(2,1)}) %reduce-scatter.6.cloned.1.call-update) | async-done | bytes 3145744 | tf_op jit(solution)/shard_map/reduce_scatter | solution.py:291
  925.6 4.3 all-gather.5
  931.9 5.5 fusion.37
  937.4 7.1 all-reduce.15
  944.9 35.7 %all-reduce.13 = (bf16[512]{0:T(512)(128)(2,1)S(1)}, bf16[512]{0:T(512)(128)(2,1)S(1)}, bf16[512]{0:T(512)(128)(2,1)S(1)}, bf16[512]{0:T(512)(128)(2,1)S(1)}, bf...) all-reduce(bf16[512]{0:T(512)(128)(2,1)S(1)} %dynamic-slice.1, ...), channel_id=1, replica_groups=mesh['ctx'=16,'fsdp'=2] {'ctx'}, use_global_device_ids=true, to_apply=%region_23.24 | all-reduce | flops 4608 | bytes 18432 | tf_op jit(solution)/shard_map/psum | solution.py:344
  985.0 140.8 %all-reduce.18.cloned.1.call-done = (bf16[512,1024]{1,0:T(8,128)(2,1)}, bf16[512,4096]{1,0:T(8,128)(2,1)}, bf16[2048,1024]{1,0:T(8,128)(2,1)}, bf16[128,2048]{1,0:T(8,128)(2,1)}) async-done(((bf16[512,1024]{1,0:T(8,128)(2,1)}, bf16[512,4096]{1,0:T(8,128)(2,1)}, bf16[2048,1024]{1,0:T(8,128)(2,1)}, bf16[128,2048]{1,0:T(8,128)(2,1)}), (bf16[512,1024]{1,0:T(8,128)(2,1)}, bf16[512,4096]{1,0:T(8,128)(2,1)}, ...) | async-done | bytes 9961488 | tf_op jit(solution)/shard_map/psum | solution.py:340
  1125.8 2.8 convert_element_type.285
  1128.6 8.2 convert_element_type.287
  1136.8 4.4 convert_element_type.289
  1142.3 231.9 %all-gather.35.cloned.1.call-done = bf16[8192,3072]{1,0:T(8,128)(2,1)} async-done(((bf16[512,3072]{1,0:T(8,128)(2,1)}), bf16[8192,3072]{1,0:T(8,128)(2,1)}) %all-gather.35.cloned.1.call-update) | async-done | bytes 50331664 | tf_op jit(solution)/shard_map/all_gather | solution.py:339
  1374.2 17.0 %reduce_sum.170 = bf16[512,3072]{1,0:T(8,128)(2,1)S(1)} reduce(bf16[16,512,3072]{2,1,0:T(8,128)(2,1)} %bitcast.150, bf16[]{:T(256)} %constant.121.clone.1), dimensions={0}, to_apply=%region_12.13 | reduce | flops 23592960 | bytes 53477376 | tf_op jit(solution)/shard_map/reduce_sum | solution.py:339
  1391.2 3.5 convert_element_type.283
  (245 shorter events, 45.9 us)
Async XLA Ops:
  7.2 8.7 copy-start.52
  7.2 13.8 copy-start.4
  7.2 26.4 %all-gather.17.cloned.1.call-start = ((), (), s32[]{:S(2)}) async-start(), calls=%async_computation.5 | async-start | bytes 1572864 | tf_op jit(solution)/shard_map/all_gather | solution.py:101
  7.9 107.7 %all-gather.19.cloned.1.call-start = ((), (), s32[]{:S(2)}) async-start(), calls=%async_computation.6 | async-start | bytes 9437184 | tf_op jit(solution)/shard_map/all_gather | solution.py:97
  8.7 172.0 %all-gather.21.cloned.1.call-start = ((), (), s32[]{:S(2)}) async-start(), calls=%async_computation.7 | async-start | bytes 4456448 | tf_op jit(solution)/shard_map/all_gather | solution.py:154
  20.3 15.7 %copy-start.27 = (f32[2,1,512]{2,1,0:T(1,128)}, f32[2,1,512]{2,1,0:T(1,128)S(1)}, u32[]{:S(2)}) copy-start(f32[2,1,512]{2,1,0:T(1,128)S(1)} %convert_element_type.305) | copy-start | bytes 12292
  20.9 14.9 %copy-start.36 = (s32[128]{0:T(128)}, s32[128]{0:T(128)S(1)}, u32[]{:S(2)}) copy-start(s32[128]{0:T(128)S(1)} %get-tuple-element.43) | copy-start | bytes 1540
  21.1 98.3 %copy-start.43 = (f32[128]{0:T(128)}, f32[128]{0:T(128)S(1)}, u32[]{:S(2)}) copy-start(f32[128]{0:T(128)S(1)} %broadcast_multiply_fusion.1) | copy-start | bytes 1540
  21.3 98.1 %copy-start.49 = (f32[128]{0:T(128)}, f32[128]{0:T(128)S(1)}, u32[]{:S(2)}) copy-start(f32[128]{0:T(128)S(1)} %fusion.78) | copy-start | bytes 1540
  22.1 102.4 %copy-start.23 = (f32[128,32]{0,1:T(8,128)}, f32[128,32]{0,1:T(8,128)S(1)}, u32[]{:S(2)}) copy-start(f32[128,32]{0,1:T(8,128)S(1)} %get-tuple-element.64) | copy-start | bytes 49156
  127.3 104.7 %all-gather.23.cloned.1.call-start = ((), (), s32[]{:S(2)}) async-start(), calls=%async_computation.8 | async-start | bytes 4456448 | tf_op jit(solution)/shard_map/all_gather | solution.py:155
  128.1 137.0 %all-gather.25.cloned.1.call-start = ((), (), s32[]{:S(2)}) async-start(), calls=%async_computation.9 | async-start | bytes 3145728 | tf_op jit(solution)/shard_map/all_gather | solution.py:98
  128.7 241.8 %all-gather.27.cloned.1.call-start = ((), (), s32[]{:S(2)}) async-start(), calls=%async_computation.10 | async-start | bytes 12582912 | tf_op jit(solution)/shard_map/all_gather | solution.py:99
  129.3 10.1 copy-start.54
  129.3 14.5 %copy-start.37 = (s32[128]{0:T(128)S(1)}, s32[128]{0:T(128)}, u32[]{:S(2)}) copy-start(s32[128]{0:T(128)} %copy-done.36) | copy-start | bytes 1540
  129.3 14.7 %copy-start.18 = (bf16[128,16,1,32]{0,3,2,1:T(8,128)(2,1)S(1)}, bf16[128,16,1,32]{0,3,2,1:T(8,128)(2,1)}, u32[]{:S(2)}) copy-start(bf16[128,16,1,32]{0,3,2,1:T(8,128)(2,1)} %get-tuple-element.61) | copy-start | bytes 393220
  129.3 346.8 %all-gather.29.cloned.1.call-start = ((), (), s32[]{:S(2)}) async-start(), calls=%async_computation.11 | async-start | bytes 12582912 | tf_op jit(solution)/shard_map/all_gather | solution.py:100
  130.1 416.8 %all-gather.31.cloned.1.call-start = ((), (), s32[]{:S(2)}) async-start(), calls=%async_computation.12 | async-start | bytes 4456448 | tf_op jit(solution)/shard_map/all_gather | solution.py:251
  144.8 439.1 %all-gather.33.cloned.1.call-start = ((), (), s32[]{:S(2)}) async-start(), calls=%async_computation.13 | async-start | bytes 4456448 | tf_op jit(solution)/shard_map/all_gather | solution.py:252
  251.8 118.7 %copy-start.14 = (bf16[128,16,64]{0,2,1:T(8,128)(2,1)}, bf16[128,16,64]{0,2,1:T(8,128)(2,1)S(1)}, u32[]{:S(2)}) copy-start(bf16[128,16,64]{0,2,1:T(8,128)(2,1)S(1)} %get-tuple-element.68) | copy-start | bytes 786436
  251.8 118.7 %copy-start.29 = (f32[4096]{0:T(1024)S(1)}, f32[4096]{0:T(1024)}, u32[]{:S(2)}) copy-start(f32[4096]{0:T(1024)} %convert_element_type.266) | copy-start | bytes 49156
  267.2 223.2 %copy-start.32 = (f32[128]{0:T(128)}, f32[128]{0:T(128)S(1)}, u32[]{:S(2)}) copy-start(f32[128]{0:T(128)S(1)} %broadcast_multiply_fusion) | copy-start | bytes 1540
  267.4 223.0 %copy-start.34 = (f32[128]{0:T(128)}, f32[128]{0:T(128)S(1)}, u32[]{:S(2)}) copy-start(f32[128]{0:T(128)S(1)} %fusion.79) | copy-start | bytes 1540
  370.5 105.6 %copy-start.30 = (f32[128]{0:T(128)S(1)}, f32[128]{0:T(128)}, u32[]{:S(2)}) copy-start(f32[128]{0:T(128)} %get-tuple-element.42) | copy-start | bytes 1540
  476.1 10.8 copy-start.2
  494.6 146.3 %reduce-scatter.8.cloned.1.call-start = ((), (), s32[]{:S(2)}) async-start(), calls=%async_computation.15 | async-start | bytes 3145728 | tf_op jit(solution)/shard_map/reduce_scatter | solution.py:294
  571.9 18.5 %copy-start.19 = (pred[2048,128]{1,0:T(8,128)(4,1)S(1)}, pred[2048,128]{1,0:T(8,128)(4,1)}, u32[]{:S(2)}) copy-start(pred[2048,128]{1,0:T(8,128)(4,1)} %broadcast_compare_fusion) | copy-start | bytes 786436
  571.9 18.5 %copy-start.26 = (f32[2048,16]{0,1:T(8,128)S(1)}, f32[2048,16]{0,1:T(8,128)}, u32[]{:S(2)}) copy-start(f32[2048,16]{0,1:T(8,128)} %all_gather.77) | copy-start | bytes 393220
  571.9 69.6 %reduce-scatter.14.cloned.1.call-start = ((), (), s32[]{:S(2)}) async-start(), calls=%async_computation.18 | async-start | bytes 1572864 | tf_op jit(solution)/shard_map/reduce_scatter | solution.py:303
  590.4 15.9 %copy-start.1 = (bf16[2048,1024]{0,1:T(8,128)(2,1)S(1)}, bf16[2048,1024]{0,1:T(8,128)(2,1)}, u32[]{:S(2)}) copy-start(bf16[2048,1024]{0,1:T(8,128)(2,1)} %all-gather.31.cloned.1.call-done) | copy-start | bytes 12582916
  590.4 19.1 %slice-start.2 = ((s8[16777216]{0:T(1024)(128)(4,1)}), s8[4194304]{0:T(1024)(128)(4,1)S(1)}, s32[]{:S(2)}) async-start(s8[16777216]{0:T(1024)(128)(4,1)} %bitcast.155), calls=%async_computation.23 | async-start | bytes 8388608
  590.4 19.1 %slice-start.3 = ((s8[16777216]{0:T(1024)(128)(4,1)}), s8[4194304]{0:T(1024)(128)(4,1)S(1)}, s32[]{:S(2)}) async-start(s8[16777216]{0:T(1024)(128)(4,1)} %bitcast.155), calls=%async_computation.24 | async-start | bytes 8388608
  590.4 19.1 %slice-start.4 = ((s8[16777216]{0:T(1024)(128)(4,1)}), s8[4194304]{0:T(1024)(128)(4,1)S(1)}, s32[]{:S(2)}) async-start(s8[16777216]{0:T(1024)(128)(4,1)} %bitcast.155), calls=%async_computation.25 | async-start | bytes 8388608
  606.3 10.8 slice-start
  609.5 7.5 slice-start.1
  609.6 7.5 copy-start.28
  609.6 7.5 copy-start.44
  622.3 121.2 %reduce-scatter.10.cloned.1.call-start = ((), (), s32[]{:S(2)}) async-start(), calls=%async_computation.16 | async-start | bytes 12582912 | tf_op jit(solution)/shard_map/reduce_scatter | solution.py:297
  628.4 217.3 %reduce-scatter.12.cloned.1.call-start = ((), (), s32[]{:S(2)}) async-start(), calls=%async_computation.17 | async-start | bytes 12582912 | tf_op jit(solution)/shard_map/reduce_scatter | solution.py:300
  635.2 290.4 %reduce-scatter.6.cloned.1.call-start = ((), (), s32[]{:S(2)}) async-start(), calls=%async_computation.14 | async-start | bytes 9437184 | tf_op jit(solution)/shard_map/reduce_scatter | solution.py:291
  640.8 485.0 %all-reduce.18.cloned.1.call-start = ((), (), s32[]{:S(2)}) async-start(), calls=%async_computation.20 | async-start | bytes 19922944 | tf_op jit(solution)/shard_map/psum | solution.py:340
  845.8 79.8 %copy-start.55 = (bf16[512]{0:T(512)(128)(2,1)S(1)}, bf16[512]{0:T(512)(128)(2,1)}, u32[]{:S(2)}) copy-start(bf16[512]{0:T(512)(128)(2,1)} %param.26) | copy-start | bytes 3076
  845.8 84.2 %copy-start.59 = (u32[32]{0:T(128)S(1)}, u32[32]{0:T(128)}, u32[]{:S(2)}) copy-start(u32[32]{0:T(128)} %constant.143) | copy-start | bytes 388
  845.8 528.4 %all-gather.35.cloned.1.call-start = ((), (), s32[]{:S(2)}) async-start(), calls=%async_computation.19 | async-start | bytes 53477376 | tf_op jit(solution)/shard_map/all_gather | solution.py:339
  931.9 52.2 %copy-start.6 = (f32[128,1024]{1,0:T(8,128)S(1)}, f32[128,1024]{1,0:T(8,128)}, u32[]{:S(2)}) copy-start(f32[128,1024]{1,0:T(8,128)} %copy-done.5) | copy-start | bytes 1572868
  931.9 52.2 %copy-start.13 = (f32[128,1024]{1,0:T(8,128)S(1)}, f32[128,1024]{1,0:T(8,128)}, u32[]{:S(2)}) copy-start(f32[128,1024]{1,0:T(8,128)} %get-tuple-element.47) | copy-start | bytes 1572868
  931.9 52.2 %copy-start.48 = (f32[128]{0:T(128)S(1)}, f32[128]{0:T(128)}, u32[]{:S(2)}) copy-start(f32[128]{0:T(128)} %copy-done.47) | copy-start | bytes 1540
  1128.6 8.2 copy-start.7
  (34 other events, 100.5 us)
Sparse Core Ops, SparseCore 0:
  9.6 23.9 all-gather.16
  35.2 80.4 all-gather.18
  127.4 53.2 all-gather.20
  183.3 48.7 all-gather.22
  233.4 31.5 all-gather.24
  266.5 103.9 all-gather.26
  372.0 103.9 all-gather.28
  478.8 54.1 all-gather.30
  535.2 48.7 all-gather.32
  586.6 30.2 reduce-scatter.7
  622.4 19.0 reduce-scatter.13
  644.2 99.2 reduce-scatter.9
  746.4 99.2 reduce-scatter.11
  848.5 77.0 reduce-scatter.5
  930.1 195.6 all-reduce.17
  1127.3 246.9 all-gather.34
